TPU v7x, 512 devices: a whole 4x8x8 slice. The times are simulated.
512 devices in a mesh: seq: 16 (over y_lo, z), clus: 32 (over x, y_hi, core).
Axes of the slice: x: 4, y: 8 (y_hi: 4, y_lo: 2; y = y_hi * 2 + y_lo), z: 8, core: 2. Of those that a mesh axis runs over, the one named last changes fastest.
Arguments:
- node_feats: bfloat16 [32, 2048, 1024], P('clus', 'seq'), may hold values from -24 to 24
- qkv_weight: bfloat16 [3072, 1024], P('seq'), may hold values from -1 to 1
- block_pairs: int32 [32, 128, 2], P('clus'), may hold values from 0 to 15, as said below
- grad_out: bfloat16 [32, 2048, 1024], P('clus', 'seq'), may hold values from -6 to 6
Outputs:
- attended: bfloat16 [32, 2048, 1024], P('clus', 'seq')
- node_grad: bfloat16 [32, 2048, 1024], P('clus', 'seq')
- weight_grad: float32 [3072, 1024], P('seq')
Inputs may be any that keep to these rules, and one draw needn't show every extreme that they name: `block_pairs`: each cluster's list holds 128 distinct pairs, among them (b, b) for every block b.
All inputs are finite; a program needn't handle non-finite values.
Results may differ from a plain program's by a relative error of at most 0.023.
Values may be sent and summed in bfloat16 or wider, within the bound.
A program may use at most 64 MiB of HBM per device.

v0:
```python
import math
import jax
import jax.numpy as jnp
from jax import lax
from jax.sharding import PartitionSpec as P

HD = 64
BLOCK = 128


def block_allowed(listed, blocks):
    block_ids = jnp.arange(blocks, dtype=jnp.int32)[None, :]
    row_hot = (listed[:, 0:1] == block_ids).astype(jnp.float32)
    col_hot = (listed[:, 1:2] == block_ids).astype(jnp.float32)
    counts = jnp.dot(row_hot.T, col_hot, precision=lax.Precision.HIGHEST)
    return counts > 0.5


def expand_rows(allowed_blocks, offset, row_span):
    picked = lax.dynamic_slice_in_dim(allowed_blocks, offset // BLOCK, row_span // BLOCK, 0)
    return jnp.repeat(jnp.repeat(picked, BLOCK, axis=0), BLOCK, axis=1)


def softmax_rows(query_rows, keys_all, allowed_rows):
    scores = jnp.einsum(
        "qhe,khe->hqk", query_rows, keys_all, preferred_element_type=jnp.float32
    ) * HD ** (-0.5)
    scores = jnp.where(allowed_rows[None], scores, -jnp.inf)
    row_max = jnp.max(scores, axis=-1, keepdims=True)
    unnorm = jnp.where(allowed_rows[None], jnp.exp(scores - row_max), 0.0)
    return unnorm / jnp.sum(unnorm, axis=-1, keepdims=True)


def local(node_feats, qkv_weight, block_pairs, grad_out):
    features = node_feats[0]
    rows_dev = features.shape[0]
    node_count = rows_dev * lax.axis_size("seq")
    columns = qkv_weight.shape[0]
    heads_dev = columns // (3 * HD)
    row_span = math.gcd(node_count, 512)
    offsets = jnp.arange(node_count // row_span, dtype=jnp.int32) * row_span
    projected = lax.dot_general(
        lax.all_gather(features, "seq", axis=0, tiled=True),
        qkv_weight,
        (((1,), (1,)), ((), ())),
        preferred_element_type=jnp.float32,
    ).astype(jnp.bfloat16)
    grouped = projected.reshape(node_count, heads_dev, 3, HD)
    queries = grouped[:, :, 0]
    keys_all = grouped[:, :, 1]
    values_all = grouped[:, :, 2]
    allowed_blocks = block_allowed(block_pairs[0], node_count // BLOCK)

    def forward_block(offset):
        query_rows = lax.dynamic_slice_in_dim(queries, offset, row_span, 0)
        weights = softmax_rows(query_rows, keys_all, expand_rows(allowed_blocks, offset, row_span))
        return jnp.einsum(
            "hqk,khe->qhe",
            weights.astype(jnp.bfloat16),
            values_all,
            preferred_element_type=jnp.float32,
        ).astype(jnp.bfloat16)

    head_out = lax.map(forward_block, offsets).reshape(node_count, heads_dev * HD)
    attended = lax.all_to_all(head_out, "seq", split_axis=0, concat_axis=1, tiled=True)
    upstream = lax.all_to_all(grad_out[0], "seq", split_axis=1, concat_axis=0, tiled=True).reshape(
        node_count, heads_dev, HD
    )

    def backward_block(state_pair, offset):
        grad_keys, grad_values = state_pair
        query_rows = lax.dynamic_slice_in_dim(queries, offset, row_span, 0)
        grad_rows = lax.dynamic_slice_in_dim(upstream, offset, row_span, 0)
        weights = softmax_rows(query_rows, keys_all, expand_rows(allowed_blocks, offset, row_span))
        weights_low = weights.astype(jnp.bfloat16)
        grad_weights = jnp.einsum(
            "qhe,khe->hqk", grad_rows, values_all, preferred_element_type=jnp.float32
        )
        row_delta = jnp.sum(weights * grad_weights, axis=-1, keepdims=True)
        grad_scores = (weights * (grad_weights - row_delta) * HD ** (-0.5)).astype(jnp.bfloat16)
        grad_query = jnp.einsum(
            "hqk,khe->qhe", grad_scores, keys_all, preferred_element_type=jnp.float32
        ).astype(jnp.bfloat16)
        grad_keys = grad_keys + jnp.einsum(
            "hqk,qhe->khe", grad_scores, query_rows, preferred_element_type=jnp.float32
        )
        grad_values = grad_values + jnp.einsum(
            "hqk,qhe->khe", weights_low, grad_rows, preferred_element_type=jnp.float32
        )
        return ((grad_keys, grad_values), grad_query)

    zeros_acc = jnp.zeros((node_count, heads_dev, HD), jnp.float32)
    sums_pair, grad_query = lax.scan(backward_block, (zeros_acc, zeros_acc), offsets)
    grad_query = grad_query.reshape(node_count, heads_dev, HD)
    grad_proj = jnp.stack(
        [grad_query, sums_pair[0].astype(jnp.bfloat16), sums_pair[1].astype(jnp.bfloat16)], axis=2
    ).reshape(node_count, columns)
    rows_part = grad_proj
    node_grad = lax.psum_scatter(
        jnp.dot(rows_part, qkv_weight, preferred_element_type=jnp.float32).astype(jnp.bfloat16),
        "seq",
        scatter_dimension=0,
        tiled=True,
    )
    rows_part = grad_proj
    local_sum = lax.dot_general(
        rows_part,
        lax.all_gather(features, "seq", axis=0, tiled=True),
        (((0,), (0,)), ((), ())),
        preferred_element_type=jnp.float32,
    )
    weight_grad = lax.psum(local_sum.astype(jnp.bfloat16), "clus").astype(
        jnp.float32
    ) / lax.axis_size("clus")
    return (attended[None], node_grad[None], weight_grad)


def solution(mesh):
    return jax.shard_map(
        local,
        mesh=mesh,
        in_specs=(
            P("clus", "seq", None),
            P("seq", None),
            P("clus", None, None),
            P("clus", "seq", None),
        ),
        out_specs=(P("clus", "seq", None), P("clus", "seq", None), P("seq", None)),
        check_vma=False,
    )
```

profile of v0, /device:TPU:6, one launch (start us, length us, event | category | flops | bytes accessed | tf_op | source)
XLA Modules:
  0.0 562.7 jit_solution(15509004296155294109)
XLA Ops:
  9.7 11.4 %all-to-all-start.1 = ((bf16[128,16,64]{0,2,1:T(8,128)(2,1)}), bf16[128,16,64]{0,2,1:T(8,128)(2,1)S(1)}, u32[]{:S(2)}, u32[]{:S(2)}) async-start(bf16[128,16,64]{0,2,1:T(8,128)(2,1)} %bitcast.19), calls=%async_computation.1 | async-start | bytes 524288 | tf_op jit(solution)/shard_map/all_to_all | solution.py:66
  22.2 9.6 %all-to-all-done.1 = bf16[128,16,64]{0,2,1:T(8,128)(2,1)S(1)} async-done(((bf16[128,16,64]{0,2,1:T(8,128)(2,1)}), bf16[128,16,64]{0,2,1:T(8,128)(2,1)S(1)}, u32[]{:S(2)}, u32[]{:S(2)}) %all-to-all-start.1) | async-done | bytes 262176 | tf_op jit(solution)/shard_map/all_to_all | solution.py:66
  32.8 61.0 %all-gather.3.cloned.1.call-done = bf16[1,2048,1024]{2,1,0:T(8,128)(2,1)} async-done(((bf16[1,128,1024]{2,1,0:T(8,128)(2,1)}), bf16[1,2048,1024]{2,1,0:T(8,128)(2,1)}) %all-gather.3.cloned.1.call-update) | async-done | bytes 4194320 | tf_op jit(solution)/shard_map/all_gather | solution.py:43
  93.8 3.7 fusion.44
  99.2 88.3 %while.30 = (s32[]{:T(128)}, f32[2048,1,64]{0,2,1:T(8,128)S(1)}, f32[2048,1,64]{0,2,1:T(8,128)S(1)}, bf16[4,512,1,64]{1,3,2,0:T(8,128)(2,1)}, s32[4]{0:T(128)S(1...) while((s32[]{:T(128)}, f32[2048,1,64]{0,2,1:T(8,128)S(1)}, ...), condition=%wide.region_8.9_spmd.clone, body=%wide.region_4.8_spmd.clone.sunk | while | flops 692615680 | bytes 80837776 | solution.py:93
  102.1 3.5 broadcast_in_dim.122
  110.2 3.0 multiply_reduce_fusion.2
  117.4 2.4 fusion.88
  124.2 3.5 broadcast_in_dim.122
  132.3 3.0 multiply_reduce_fusion.2
  139.5 2.4 fusion.88
  146.3 3.5 broadcast_in_dim.122
  154.4 3.0 multiply_reduce_fusion.2
  161.6 2.4 fusion.88
  168.4 3.5 broadcast_in_dim.122
  173.0 2.2 fusion.84
  176.5 3.0 multiply_reduce_fusion.2
  183.7 2.4 fusion.88
  189.0 3.9 fusion.47
  193.2 3.2 convolution_convert_fusion.1
  196.5 56.6 %while.29 = (s32[]{:T(128)}, bf16[4,512,1,64]{1,3,2,0:T(8,128)(2,1)S(1)}, s32[4]{0:T(128)S(1)}, pred[16,16]{1,0:T(8,128)(4,1)S(1)}, bf16[2048,1,64]{0,2,1:T(8,12...) while((s32[]{:T(128)}, ...), condition=%wide.region_3.4_spmd, body=%wide.region_0.3_spmd.sunk | while | flops 283147264 | bytes 17459756 | solution.py:64
  199.8 3.5 broadcast_in_dim.117
  208.1 2.6 fusion.77
  213.9 3.5 broadcast_in_dim.117
  222.2 2.6 fusion.77
  228.1 3.5 broadcast_in_dim.117
  236.4 2.6 fusion.77
  242.2 3.5 broadcast_in_dim.117
  250.5 2.6 fusion.77
  254.2 3.9 all-to-all-start
  258.1 203.0 %all-reduce.2.cloned.1.call-done = bf16[192,1024]{1,0:T(8,128)(2,1)} async-done(((bf16[192,1024]{1,0:T(8,128)(2,1)}), bf16[192,1024]{1,0:T(8,128)(2,1)}) %all-reduce.2.cloned.1.call-update) | async-done | bytes 393232 | tf_op jit(solution)/shard_map/psum | solution.py:112
  463.9 92.3 %reduce-scatter.2.cloned.1.call-done = bf16[128,1024]{1,0:T(8,128)(2,1)} async-done(((bf16[2048,1024]{1,0:T(8,128)(2,1)}), bf16[128,1024]{1,0:T(8,128)(2,1)}) %reduce-scatter.2.cloned.1.call-update) | async-done | bytes 262160 | tf_op jit(solution)/shard_map/reduce_scatter | solution.py:99
  (96 shorter events, 65.8 us)
Async XLA Ops:
  7.2 86.7 %copy-start = (bf16[192,1024]{1,0:T(8,128)(2,1)S(1)}, bf16[192,1024]{1,0:T(8,128)(2,1)}, u32[]{:S(2)}) copy-start(bf16[192,1024]{1,0:T(8,128)(2,1)} %param.9) | copy-start | bytes 1179652
  7.2 86.7 %all-gather.3.cloned.1.call-start = ((), (), s32[]{:S(2)}) async-start(), calls=%async_computation.5 | async-start | bytes 4456448 | tf_op jit(solution)/shard_map/all_gather | solution.py:43
  9.7 22.1 %all-to-all-start.1 = ((bf16[128,16,64]{0,2,1:T(8,128)(2,1)}), bf16[128,16,64]{0,2,1:T(8,128)(2,1)S(1)}, u32[]{:S(2)}, u32[]{:S(2)}) async-start(bf16[128,16,64]{0,2,1:T(8,128)(2,1)} %bitcast.19), calls=%async_computation.1 | async-start | bytes 524288 | tf_op jit(solution)/shard_map/all_to_all | solution.py:66
  21.1 439.9 %all-reduce.2.cloned.1.call-start = ((), (), s32[]{:S(2)}) async-start(), calls=%async_computation.4 | async-start | bytes 786432 | tf_op jit(solution)/shard_map/psum | solution.py:112
  113.3 2.0 copy-start.1
  115.8 4.0 copy-start.2
  135.4 2.0 copy-start.1
  137.9 4.0 copy-start.2
  157.5 2.0 copy-start.1
  160.0 4.0 copy-start.2
  179.6 2.0 copy-start.1
  182.1 4.0 copy-start.2
  192.9 363.3 %reduce-scatter.2.cloned.1.call-start = ((), (), s32[]{:S(2)}) async-start(), calls=%async_computation.3 | async-start | bytes 4456448 | tf_op jit(solution)/shard_map/reduce_scatter | solution.py:99
  254.2 208.8 %all-to-all-start = ((bf16[16,128,64]{1,2,0:T(8,128)(2,1)}), bf16[16,128,64]{1,2,0:T(8,128)(2,1)S(1)}, u32[]{:S(2)}, u32[]{:S(2)}) async-start(bf16[16,128,64]{1,2,0:T(8,128)(2,1)} %copy.18), calls=%async_computation | async-start | bytes 524288 | tf_op jit(solution)/shard_map/all_to_all | solution.py:65
Sparse Core Ops, SparseCore 0:
  10.1 83.7 all-gather.2
  193.1 267.9 all-reduce.1
  464.5 91.6 reduce-scatter.1
where the time goes:
time: 564 us; the launch traced here: 563 us
  waiting for transfers between devices  367 us (65%)
  matrix products  72.6 us (13%)
  local copies, waits for them, and re-layouts  49.3 us (9%)
  loops' own time  29.3 us (5%)
  starting transfers between devices  15.6 us (3%)
  other arithmetic  15.5 us (3%)
  between operations  13.9 us (2%)
    psum x1, waiting for transfers between devices, local(): lax.psum(local_sum.astype(jnp.bfloat16), 'clus').astype(jnp.float32)  203 us
    reduce_scatter x1, waiting for transfers between devices, local(): lax.psum_scatter(jnp.dot(rows_part, qkv_weight, preferred_element_type=jn...  92.3 us
    all_gather x1, waiting for transfers between devices, local(): lax.all_gather(features, 'seq', axis=0, tiled=True)  61 us
    broadcast_in_dim x16, local copies, waits for them, and re-layouts, expand_rows(): return jnp.repeat(jnp.repeat(picked, BLOCK, axis=0), BLOCK, axis=1)  27.9 us
    dot_general x8, matrix products, softmax_rows(): jnp.einsum('qhe,khe->hqk', query_rows, keys_all, preferred_element_type=j...  17.3 us
    another operation x1, loops' own time, local(): lax.map(forward_block, offsets).reshape(node_count, heads_dev * HD)  15.5 us
    another operation x1, loops' own time, local(): lax.scan(backward_block, (zeros_acc, zeros_acc), offsets)  13.8 us
    dot_general x4, matrix products, backward_block(): jnp.einsum('qhe,khe->hqk', grad_rows, values_all, preferred_element_type=...  12.1 us
  transfers between devices with their start and end apart: 5, of which 4 were waited for; matrix products, arithmetic and copies ran while one was open for 9% of the time, Pallas kernels for 0%

commit v1 on v0

--- a/solution.py
+++ b/solution.py
@@ -39,8 +39,15 @@
     heads_dev = columns // (3 * HD)
     row_span = math.gcd(node_count, 512)
     offsets = jnp.arange(node_count // row_span, dtype=jnp.int32) * row_span
+
+    def create_loops(t0, array_dim=0):
+        return jnp.concatenate(
+            lax.all_to_all(jnp.stack([t0 for _ in range(lax.axis_size("seq"))], 0), "seq", 0, 0),
+            array_dim,
+        )
+
     projected = lax.dot_general(
-        lax.all_gather(features, "seq", axis=0, tiled=True),
+        create_loops(features),
         qkv_weight,
         (((1,), (1,)), ((), ())),
         preferred_element_type=jnp.float32,

time: 564 us -> 632 us (1.12)
  waiting for transfers between devices: 367 us -> 417 us
  blocking collectives: 0 us -> 21.9 us
    all_to_all x1, waiting for transfers between devices: 9.6 us -> 120 us  [create_loops(): lax.all_to_all(jnp.stack([t0 for _ in range(lax.axis_size('seq'))], 0), '...]
    all_gather x1, waiting for transfers between devices: 61 us -> 0.02 us  [local(): lax.all_gather(features, 'seq', axis=0, tiled=True)]
    all_to_all x0 -> x1, blocking collectives: none -> 21.9 us  [local(): lax.all_to_all(grad_out[0], 'seq', split_axis=1, concat_axis=0, tiled=True)]
    all_to_all x1, starting transfers between devices: 11.4 us -> 4.67 us  [create_loops(): lax.all_to_all(jnp.stack([t0 for _ in range(lax.axis_size('seq'))], 0), '...]
  transfers between devices with their start and end apart: 5 -> 5, of which waited for: 4 -> 3; matrix products, arithmetic and copies ran while one was open for 9% -> 19% of each run, Pallas kernels for 0% -> 0%
where the time goes in v1:
time: 632 us; the launch traced here: 631 us
  waiting for transfers between devices  417 us (66%)
  matrix products  72.6 us (11%)
  local copies, waits for them, and re-layouts  51.1 us (8%)
  loops' own time  29 us (5%)
  blocking collectives  21.9 us (3%)
  other arithmetic  15.5 us (2%)
  between operations  13.9 us (2%)
  starting transfers between devices  9.79 us (2%)
    psum x1, waiting for transfers between devices, local(): lax.psum(local_sum.astype(jnp.bfloat16), 'clus').astype(jnp.float32)  205 us
    all_to_all x1, waiting for transfers between devices, create_loops(): lax.all_to_all(jnp.stack([t0 for _ in range(lax.axis_size('seq'))], 0), '...  120 us
    reduce_scatter x1, waiting for transfers between devices, local(): lax.psum_scatter(jnp.dot(rows_part, qkv_weight, preferred_element_type=jn...  92.3 us
    broadcast_in_dim x16, local copies, waits for them, and re-layouts, expand_rows(): return jnp.repeat(jnp.repeat(picked, BLOCK, axis=0), BLOCK, axis=1)  27.9 us
    all_to_all x1, blocking collectives, local(): lax.all_to_all(grad_out[0], 'seq', split_axis=1, concat_axis=0, tiled=True)  21.9 us
    dot_general x8, matrix products, softmax_rows(): jnp.einsum('qhe,khe->hqk', query_rows, keys_all, preferred_element_type=j...  17.3 us
    another operation x1, loops' own time, local(): lax.map(forward_block, offsets).reshape(node_count, heads_dev * HD)  15.4 us
    another operation x1, loops' own time, local(): lax.scan(backward_block, (zeros_acc, zeros_acc), offsets)  13.6 us
  transfers between devices with their start and end apart: 5, of which 3 were waited for; matrix products, arithmetic and copies ran while one was open for 19% of the time, Pallas kernels for 0%

profile of v1, /device:TPU:6, one launch (start us, length us, event | category | flops | bytes accessed | tf_op | source)
XLA Modules:
  0.0 631.0 jit_solution(126770877168843011)
XLA Ops:
  8.4 21.9 %all_to_all.37 = bf16[128,16,64]{0,2,1:T(8,128)(2,1)S(1)} all-to-all(bf16[128,16,64]{0,2,1:T(8,128)(2,1)S(1)} %bitcast.217), channel_id=1, replica_groups=mesh['seq'=16,'clus'=32] {'seq'}, dimensions={1} | all-to-all | bytes 524288 | tf_op jit(solution)/shard_map/all_to_all | solution.py:73
  30.3 3.4 stack.12
  33.7 4.7 all-to-all-start
  40.5 119.7 %all-to-all-done = bf16[16,128,1024]{2,1,0:T(8,128)(2,1)} async-done(((bf16[16,128,1024]{2,1,0:T(8,128)(2,1)}), bf16[16,128,1024]{2,1,0:T(8,128)(2,1)}, u32[]{:S(2)}, u32[]{:S(2)}) %all-to-all-start) | async-done | bytes 4194336 | tf_op jit(solution)/shard_map/all_to_all | solution.py:45
  160.2 3.7 convolution_convert_fusion.2
  165.6 88.0 %while.30 = (s32[]{:T(128)}, f32[2048,1,64]{0,2,1:T(8,128)S(1)}, f32[2048,1,64]{0,2,1:T(8,128)S(1)}, bf16[4,512,1,64]{1,3,2,0:T(8,128)(2,1)}, s32[4]{0:T(128)S(1...) while((s32[]{:T(128)}, f32[2048,1,64]{0,2,1:T(8,128)S(1)}, ...), condition=%wide.region_8.9_spmd.clone, body=%wide.region_4.8_spmd.clone.sunk | while | flops 692615680 | bytes 80837776 | solution.py:100
  168.4 3.5 broadcast_in_dim.122
  176.5 3.0 multiply_reduce_fusion.2
  183.7 2.4 fusion.84
  190.4 3.5 broadcast_in_dim.122
  198.5 3.0 multiply_reduce_fusion.2
  205.7 2.4 fusion.84
  212.4 3.5 broadcast_in_dim.122
  220.5 3.0 multiply_reduce_fusion.2
  227.8 2.4 fusion.84
  234.4 3.5 broadcast_in_dim.122
  242.6 3.0 multiply_reduce_fusion.2
  249.7 2.4 fusion.84
  255.1 3.9 fusion.42
  259.2 3.2 convolution_convert_fusion.1
  262.5 56.4 %while.29 = (s32[]{:T(128)}, bf16[4,512,1,64]{1,3,2,0:T(8,128)(2,1)S(1)}, s32[4]{0:T(128)S(1)}, pred[16,16]{1,0:T(8,128)(4,1)S(1)}, bf16[2048,1,64]{0,2,1:T(8,12...) while((s32[]{:T(128)}, ...), condition=%wide.region_3.4_spmd, body=%wide.region_0.3_spmd.sunk | while | flops 283147264 | bytes 17459756 | solution.py:71
  265.7 3.5 broadcast_in_dim.117
  274.0 2.6 fusion.73
  279.8 3.5 broadcast_in_dim.117
  288.1 2.6 fusion.73
  294.0 3.5 broadcast_in_dim.117
  302.3 2.6 fusion.73
  308.1 3.5 broadcast_in_dim.117
  316.4 2.6 fusion.73
  320.0 4.8 all-to-all-start.1
  324.9 204.5 %all-reduce.2.cloned.1.call-done = bf16[192,1024]{1,0:T(8,128)(2,1)} async-done(((bf16[192,1024]{1,0:T(8,128)(2,1)}), bf16[192,1024]{1,0:T(8,128)(2,1)}) %all-reduce.2.cloned.1.call-update) | async-done | bytes 393232 | tf_op jit(solution)/shard_map/psum | solution.py:119
  532.2 92.3 %reduce-scatter.2.cloned.1.call-done = bf16[128,1024]{1,0:T(8,128)(2,1)} async-done(((bf16[2048,1024]{1,0:T(8,128)(2,1)}), bf16[128,1024]{1,0:T(8,128)(2,1)}) %reduce-scatter.2.cloned.1.call-update) | async-done | bytes 262160 | tf_op jit(solution)/shard_map/reduce_scatter | solution.py:106
  (100 shorter events, 66.3 us)
Async XLA Ops:
  7.2 153.0 %copy-start = (bf16[192,1024]{1,0:T(8,128)(2,1)S(1)}, bf16[192,1024]{1,0:T(8,128)(2,1)}, u32[]{:S(2)}) copy-start(bf16[192,1024]{1,0:T(8,128)(2,1)} %param.9) | copy-start | bytes 1179652
  33.7 5.5 copy-start.3
  33.7 126.5 %all-to-all-start = ((bf16[16,128,1024]{2,1,0:T(8,128)(2,1)}), bf16[16,128,1024]{2,1,0:T(8,128)(2,1)}, u32[]{:S(2)}, u32[]{:S(2)}) async-start(bf16[16,128,1024]{2,1,0:T(8,128)(2,1)} %stack.12), calls=%async_computation | async-start | bytes 8388608 | tf_op jit(solution)/shard_map/all_to_all | solution.py:45
  38.4 216.7 %all-gather.3.cloned.1.call-start = ((), (), s32[]{:S(2)}) async-start(), calls=%async_computation.6 | async-start | bytes 4456448 | tf_op jit(solution)/shard_map/all_gather | solution.py:115
  39.1 490.3 %all-reduce.2.cloned.1.call-start = ((), (), s32[]{:S(2)}) async-start(), calls=%async_computation.5 | async-start | bytes 786432 | tf_op jit(solution)/shard_map/psum | solution.py:119
  179.5 2.0 copy-start.1
  182.1 4.0 copy-start.2
  201.6 2.0 copy-start.1
  204.1 4.0 copy-start.2
  223.6 2.0 copy-start.1
  226.1 4.0 copy-start.2
  245.6 2.0 copy-start.1
  248.1 4.0 copy-start.2
  259.0 365.5 %reduce-scatter.2.cloned.1.call-start = ((), (), s32[]{:S(2)}) async-start(), calls=%async_computation.4 | async-start | bytes 4456448 | tf_op jit(solution)/shard_map/reduce_scatter | solution.py:106
  320.0 211.3 %all-to-all-start.1 = ((bf16[16,128,64]{1,2,0:T(8,128)(2,1)}), bf16[16,128,64]{1,2,0:T(8,128)(2,1)S(1)}, u32[]{:S(2)}, u32[]{:S(2)}) async-start(bf16[16,128,64]{1,2,0:T(8,128)(2,1)} %copy.18), calls=%async_computation.1 | async-start | bytes 524288 | tf_op jit(solution)/shard_map/all_to_all | solution.py:72
Sparse Core Ops, SparseCore 0:
  41.3 154.9 all-gather.2
  259.1 270.2 all-reduce.1
  532.8 91.6 reduce-scatter.1
